TPU v7x, 512 devices: a whole 4x4x16 slice. The times are simulated.
512 devices in a mesh: row: 32 (over y, z_hi, core), col: 16 (over z_lo, x).
Axes of the slice: x: 4, y: 4, z: 16 (z_hi: 4, z_lo: 4; z = z_hi * 4 + z_lo), core: 2. Of those that a mesh axis runs over, the one named last changes fastest.
Arguments:
- forcing_terms: float32 [32, 16, 2, 32, 128], P('row', 'col'), may hold values from -6 to 6
- diagonal_reciprocal: float32 [32, 16, 2, 128, 128], P('row', 'col'), may hold values from -0.5 to 0.5
- stiffness_submatrix: float32 [32, 16, 32, 128, 128], P('row', 'col'), may hold values from -0.1875 to 0.1875
- stiffness_source_index: int32 [32, 16, 32], P('row', 'col'), may hold values from 0 to 31
- stiffness_target_index: int32 [32, 16, 32], P('row', 'col'), may hold values from 0 to 63
- stiffness_nonzero_tally: int32 [32, 16], P('row', 'col'), may hold values from 1 to 32, as said below
- interpolant_submatrix: float32 [32, 16, 16, 128, 128], P('row', 'col'), may hold values from -0.0625 to 0.0625
- interpolant_cluster_index: int32 [32, 16, 16], P('row', 'col'), may hold values from 0 to 1
- interpolant_target_index: int32 [32, 16, 16], P('row', 'col'), may hold values from 0 to 63
- interpolant_nonzero_tally: int32 [32, 16], P('row', 'col'), may hold values from 1 to 16, as said below
- provisional_interpolant: float32 [32, 16, 2, 128], P('row', 'col'), may hold values from 0.2 to 1
- cluster_label: int32 [32, 16, 2, 128], P('row', 'col'), may hold values from 0 to 255
Outputs:
- relaxed_iterate: float32 [32, 16, 2, 32, 128], P('row', 'col')
- residual: float32 [32, 16, 2, 32, 128], P('row', 'col')
- coarse: float32 [32, 2, 32, 128], P('row')
Inputs may be any that keep to these rules, and one draw needn't show every extreme that they name: `stiffness_nonzero_tally`: tile slots at or past the count are unused; some pair has all 32 slots live in every draw. `interpolant_nonzero_tally`: tile slots at or past the count are unused; some pair has all 16 slots live in every draw.
All inputs are finite; a program needn't handle non-finite values.
Results may differ from a plain program's by a relative error of at most 0.0003.
Values sent between devices are 32-bit elements; how exact they have to be, the bound alone decides.
No kernel may reach another device: no remote copies, remote signals or barrier semaphores. Data moves between devices by JAX's collectives and lax.ppermute only.
A program may use at most 64 MiB of HBM per device.

v0:
```python
import jax
import jax.numpy as jnp
from jax import lax
from jax.sharding import PartitionSpec as P

omega = 0.7
highest = lax.Precision.HIGHEST
tile_group = 8


def loop_tiles(blocks, stiffness_submatrices, rows, cols, low, high, nout):
    nrhs = blocks.shape[1]
    width = blocks.shape[2]

    def add_group(index, total):
        start = index * tile_group
        piece = lax.dynamic_slice_in_dim(stiffness_submatrices, start, tile_group, 0)
        row_ids = lax.dynamic_slice_in_dim(rows, start, tile_group, 0)
        col_ids = lax.dynamic_slice_in_dim(cols, start, tile_group, 0)
        slots = start + jnp.arange(tile_group)
        live = ((slots >= low) & (slots < high)).astype(jnp.float32)
        inputs = jnp.take(blocks, col_ids, axis=0)
        product = jnp.einsum("ska,sab->skb", inputs, piece, precision=highest)
        onehot = (row_ids[:, None] == jnp.arange(nout)[None, :]).astype(jnp.float32) * live[:, None]
        return total + jnp.einsum("so,skb->okb", onehot, product, precision=highest)

    starting_guess = low // tile_group
    last = (high + tile_group - 1) // tile_group
    empty = jnp.zeros((nout, nrhs, width), jnp.float32)
    return lax.fori_loop(starting_guess, last, add_group, empty)


def gather_columns(vec):
    whole = lax.all_gather(vec[None, None], "row", axis=0, tiled=True)
    return whole.reshape(-1, vec.shape[1], vec.shape[2])


def precondition(vec, inverse):
    return jnp.einsum("pka,pab->pkb", vec, inverse, precision=highest)


def stiffness_product(vec, stiffness_submatrices, rows, cols, count):
    blocks = gather_columns(vec)
    ncol = lax.axis_size("col")
    pblocks = vec.shape[0]
    nout = ncol * pblocks
    partial_value = loop_tiles(blocks, stiffness_submatrices, rows, cols, jnp.int32(0), count, nout)
    partial_value = partial_value.reshape(1, ncol, pblocks, vec.shape[1], vec.shape[2])
    summed = lax.psum_scatter(partial_value, "col", scatter_dimension=1, tiled=True)
    return summed[0, 0]


def body(
    forcing_terms,
    diagonal_reciprocal,
    stiffness_submatrix,
    stiffness_source_index,
    stiffness_target_index,
    stiffness_nonzero_tally,
    interpolant_submatrix,
    interpolant_cluster_index,
    interpolant_target_index,
    interpolant_nonzero_tally,
    provisional_interpolant,
    cluster_label,
):
    source = forcing_terms[0, 0]
    inverse = diagonal_reciprocal[0, 0]
    stiffness_submatrices = stiffness_submatrix[0, 0]
    rows = stiffness_source_index[0, 0]
    cols = stiffness_target_index[0, 0]
    count = stiffness_nonzero_tally[0, 0]
    starting_guess = omega * precondition(source, inverse)
    image_field = stiffness_product(starting_guess, stiffness_submatrices, rows, cols, count)
    relaxed_iterate = starting_guess + omega * precondition(source - image_field, inverse)
    image_field = stiffness_product(relaxed_iterate, stiffness_submatrices, rows, cols, count)
    residual = source - image_field
    pblocks, nrhs, width = residual.shape
    blocks = gather_columns(residual)
    part = loop_tiles(
        blocks,
        interpolant_submatrix[0, 0],
        interpolant_cluster_index[0, 0],
        interpolant_target_index[0, 0],
        jnp.int32(0),
        interpolant_nonzero_tally[0, 0],
        pblocks,
    )
    weighted = (
        (residual * provisional_interpolant[0, 0][:, None, :])
        .transpose(1, 0, 2)
        .reshape(nrhs, pblocks * width)
    )
    onehot = (
        cluster_label[0, 0].reshape(-1)[:, None] == jnp.arange(pblocks * width)[None, :]
    ).astype(jnp.float32)
    tentative = jnp.dot(weighted, onehot, precision=highest)
    part = part + tentative.reshape(nrhs, pblocks, width).transpose(1, 0, 2)
    coarse = lax.psum(part, "col")
    return (relaxed_iterate[None, None], residual[None, None], coarse[None])


def solution(mesh):
    placed = (
        P("row", "col", None, None, None),
        P("row", "col", None, None, None),
        P("row", "col", None, None, None),
        P("row", "col", None),
        P("row", "col", None),
        P("row", "col"),
        P("row", "col", None, None, None),
        P("row", "col", None),
        P("row", "col", None),
        P("row", "col"),
        P("row", "col", None, None),
        P("row", "col", None, None),
    )
    return jax.shard_map(
        body,
        mesh=mesh,
        in_specs=placed,
        out_specs=(
            P("row", "col", None, None, None),
            P("row", "col", None, None, None),
            P("row", None, None, None),
        ),
        check_vma=False,
    )
```

profile of v0, /device:TPU:8, one launch (start us, length us, event | category | flops | bytes accessed | tf_op | source)
XLA Modules:
  0.0 539.8 jit_solution(16684769150870673594)
XLA Ops:
  7.2 0.0 copy-start
  7.2 0.0 all-gather.8.cloned.1.call-start
  7.2 0.8 copy-done
  8.1 1.6 convolution_multiply_fusion.1
  9.7 0.0 all-gather.8.cloned.1.call-update
  9.7 0.0 reduce-scatter.3.cloned.1.call-start
  10.4 76.2 %all-gather.8.cloned.1.call-done = f32[64,32,128]{2,1,0:T(8,128)} async-done(((f32[2,32,128]{2,1,0:T(8,128)}), f32[64,32,128]{2,1,0:T(8,128)}) %all-gather.8.cloned.1.call-update) | async-done | bytes 1048592 | tf_op jit(solution)/shard_map/all_gather | solution.py:34
  86.7 0.0 copy-start.3
  86.7 19.1 %while.30 = (s32[]{:T(128)}, f32[32,32,128]{2,0,1:T(8,128)S(1)}, s32[]{:T(128)}, s32[32]{0:T(128)}, s32[]{:T(128)}, /*index=5*/s32[32]{0:T(128)}, f32[64,32,128]...) while((s32[]{:T(128)}, f32[32,32,128]{2,0,1:T(8,128)S(1)}, ...), condition=%wide.region_1.3_spmd, body=%wide.region_0.2_spmd.sunk | while | flops 63080028 | bytes 2232807 | solution.py:30
  86.7 1.4 compare_and_fusion.6
  88.1 1.8 gather_fusion
  89.9 1.7 fusion.75
  91.6 0.7 dynamic_slice.46
  92.3 0.8 convolution_add_fusion.6
  93.1 1.4 compare_and_fusion.6
  94.5 1.8 gather_fusion
  96.3 1.7 fusion.75
  97.9 0.7 dynamic_slice.46
  98.7 0.8 convolution_add_fusion.6
  99.5 1.4 compare_and_fusion.6
  100.9 1.8 gather_fusion
  102.7 1.7 fusion.75
  104.3 0.7 dynamic_slice.46
  105.0 0.8 convolution_add_fusion.6
  105.9 1.1 copy.25
  107.0 0.0 reduce-scatter.3.cloned.1.call-update
  107.0 0.0 all-gather.10.cloned.1.call-start
  107.1 91.7 %reduce-scatter.3.cloned.1.call-done = f32[1,1,2,32,128]{4,3,2,1,0:T(8,128)} async-done(((f32[1,16,2,32,128]{4,3,2,1,0:T(8,128)}), f32[1,1,2,32,128]{4,3,2,1,0:T(8,128)}) %reduce-scatter.3.cloned.1.call-update) | async-done | bytes 32784 | tf_op jit(solution)/shard_map/reduce_scatter | solution.py:49
  198.8 1.6 fusion.45
  200.4 0.0 all-gather.10.cloned.1.call-update
  200.4 0.0 reduce-scatter.5.cloned.1.call-start
  200.5 68.7 %all-gather.10.cloned.1.call-done = f32[64,32,128]{2,1,0:T(8,128)} async-done(((f32[2,32,128]{2,1,0:T(8,128)}), f32[64,32,128]{2,1,0:T(8,128)}) %all-gather.10.cloned.1.call-update) | async-done | bytes 1048592 | tf_op jit(solution)/shard_map/all_gather | solution.py:34
  269.3 15.3 %while.31 = (s32[]{:T(128)}, f32[32,32,128]{2,0,1:T(8,128)S(1)}, s32[]{:T(128)}, s32[32]{0:T(128)S(1)}, s32[]{:T(128)}, /*index=5*/s32[32]{0:T(128)S(1)}, f32[64...) while((s32[]{:T(128)}, f32[32,32,128]{2,0,1:T(8,128)S(1)}, ...), condition=%wide.region_4.6_spmd, body=%wide.region_3.5_spmd.sunk | while | flops 63080028 | bytes 2232807 | solution.py:30
  269.3 0.8 compare_and_fusion.7
  270.2 1.8 gather_fusion.1
  271.9 1.7 fusion.80
  273.6 0.1 dynamic_slice.48
  273.7 0.8 convolution_add_fusion.7
  274.5 0.7 compare_and_fusion.7
  275.2 1.8 gather_fusion.1
  277.0 1.7 fusion.80
  278.7 0.1 dynamic_slice.48
  278.7 0.8 convolution_add_fusion.7
  279.6 0.7 compare_and_fusion.7
  280.3 1.8 gather_fusion.1
  282.1 1.7 fusion.80
  283.7 0.1 dynamic_slice.48
  283.8 0.8 convolution_add_fusion.7
  284.6 1.1 copy.26
  285.7 0.0 reduce-scatter.5.cloned.1.call-update
  285.8 0.0 all-gather.6.cloned.1.call-start
  285.8 90.4 %reduce-scatter.5.cloned.1.call-done = f32[1,1,2,32,128]{4,3,2,1,0:T(8,128)} async-done(((f32[1,16,2,32,128]{4,3,2,1,0:T(8,128)}), f32[1,1,2,32,128]{4,3,2,1,0:T(8,128)}) %reduce-scatter.5.cloned.1.call-update) | async-done | bytes 32784 | tf_op jit(solution)/shard_map/reduce_scatter | solution.py:49
  376.2 1.4 sub.30
  377.6 0.0 all-gather.6.cloned.1.call-update
  378.3 0.8 fusion.52
  379.2 67.5 %all-gather.6.cloned.1.call-done = f32[32,1,2,32,128]{4,3,2,1,0:T(8,128)} async-done(((f32[1,1,2,32,128]{4,3,2,1,0:T(8,128)}), f32[32,1,2,32,128]{4,3,2,1,0:T(8,128)}) %all-gather.6.cloned.1.call-update) | async-done | bytes 1048592 | tf_op jit(solution)/shard_map/all_gather | solution.py:34
  446.8 3.6 while.32
  446.8 0.7 compare_and_fusion.8
  447.5 1.8 gather_fusion.2
  449.3 0.6 fusion.85
  449.9 0.1 dynamic_slice.50
  450.0 0.3 convolution_add_fusion.8
  450.4 0.3 fusion.44
  450.7 82.6 %psum.7 = f32[1,2,32,128]{3,2,1,0:T(8,128)} all-reduce(f32[1,2,32,128]{3,2,1,0:T(8,128)S(1)} %fusion.44), channel_id=1, replica_groups=mesh['row'=32,'col'=16] {'col'}, use_global_device_ids=true, to_apply=%region_8.10 | all-reduce | flops 8192 | bytes 65536 | tf_op jit(solution)/shard_map/psum | solution.py:99
  (30 shorter events, 0.3 us)
Async XLA Ops:
  7.2 0.9 copy-start
  7.2 79.4 %all-gather.8.cloned.1.call-start = ((), (), s32[]{:S(2)}) async-start(), calls=%async_computation.5 | async-start | bytes 1081344 | tf_op jit(solution)/shard_map/all_gather | solution.py:34
  9.7 189.1 %reduce-scatter.3.cloned.1.call-start = ((), (), s32[]{:S(2)}) async-start(), calls=%async_computation.2 | async-start | bytes 557056 | tf_op jit(solution)/shard_map/reduce_scatter | solution.py:49
  86.7 112.1 %copy-start.2 = (f32[1,1,2,32,128]{4,3,2,1,0:T(8,128)S(1)}, f32[1,1,2,32,128]{4,3,2,1,0:T(8,128)}, u32[]{:S(2)}) copy-start(f32[1,1,2,32,128]{4,3,2,1,0:T(8,128)} %param.20) | copy-start | bytes 98308
  86.7 112.1 %copy-start.3 = (f32[2,32,128]{2,1,0:T(8,128)S(1)}, f32[2,32,128]{2,1,0:T(8,128)}, u32[]{:S(2)}) copy-start(f32[2,32,128]{2,1,0:T(8,128)} %convolution_multiply_fusion.1) | copy-start | bytes 98308
  105.8 163.4 %copy-start.4 = (s32[32]{0:T(128)S(1)}, s32[32]{0:T(128)}, u32[]{:S(2)}) copy-start(s32[32]{0:T(128)} %get-tuple-element.489) | copy-start | bytes 388
  105.9 163.4 %copy-start.8 = (s32[32]{0:T(128)S(1)}, s32[32]{0:T(128)}, u32[]{:S(2)}) copy-start(s32[32]{0:T(128)} %get-tuple-element.491) | copy-start | bytes 388
  107.0 162.2 %all-gather.10.cloned.1.call-start = ((), (), s32[]{:S(2)}) async-start(), calls=%async_computation.6 | async-start | bytes 1081344 | tf_op jit(solution)/shard_map/all_gather | solution.py:34
  200.4 175.8 %reduce-scatter.5.cloned.1.call-start = ((), (), s32[]{:S(2)}) async-start(), calls=%async_computation.3 | async-start | bytes 557056 | tf_op jit(solution)/shard_map/reduce_scatter | solution.py:49
  269.3 109.0 %copy-start.6 = (f32[1,1,2,128]{3,2,1,0:T(2,128)S(1)}, f32[1,1,2,128]{3,2,1,0:T(2,128)}, u32[]{:S(2)}) copy-start(f32[1,1,2,128]{3,2,1,0:T(2,128)} %param.30) | copy-start | bytes 3076
  269.3 177.4 %copy-start.1 = (f32[1,1,16,128,128]{4,3,2,1,0:T(8,128)S(1)}, f32[1,1,16,128,128]{4,3,2,1,0:T(8,128)}, u32[]{:S(2)}) copy-start(f32[1,1,16,128,128]{4,3,2,1,0:T(8,128)} %param.26) | copy-start | bytes 3145732
  269.3 177.4 %copy-start.5 = (s32[1,1,16]{2,1,0:T(1,128)S(1)}, s32[1,1,16]{2,1,0:T(1,128)}, u32[]{:S(2)}) copy-start(s32[1,1,16]{2,1,0:T(1,128)} %param.28) | copy-start | bytes 196
  269.3 177.4 %copy-start.9 = (s32[1,1,16]{2,1,0:T(1,128)S(1)}, s32[1,1,16]{2,1,0:T(1,128)}, u32[]{:S(2)}) copy-start(s32[1,1,16]{2,1,0:T(1,128)} %param.27) | copy-start | bytes 196
  285.8 160.9 %all-gather.6.cloned.1.call-start = ((), (), s32[]{:S(2)}) async-start(), calls=%async_computation.4 | async-start | bytes 1081344 | tf_op jit(solution)/shard_map/all_gather | solution.py:34
  446.7 3.6 copy-start.7
Sparse Core Ops, SparseCore 0:
  11.7 74.8 all-gather.7
  107.1 91.6 reduce-scatter.2
  202.5 66.6 all-gather.9
  285.9 90.2 reduce-scatter.4
  379.8 66.8 all-gather.5
where the time goes:
time: 541 us; the launch traced here: 540 us
  waiting for transfers between devices  395 us (73%)
  blocking collectives  82.6 us (15%)
  matrix products  19.1 us (4%)
  local copies, waits for them, and re-layouts  18.2 us (3%)
  between operations  15.3 us (3%)
  other arithmetic  9.33 us (2%)
    all_gather x3, waiting for transfers between devices, gather_columns(): whole = lax.all_gather(vec[None, None], 'row', axis=0, tiled=True)  212 us
    reduce_scatter x2, waiting for transfers between devices, stiffness_product(): lax.psum_scatter(partial_value, 'col', scatter_dimension=1, tiled=True)  182 us
    psum x1, blocking collectives, body(): coarse = lax.psum(part, 'col')  82.6 us
    gather x7, local copies, waits for them, and re-layouts, add_group(): inputs = jnp.take(blocks, col_ids, axis=0)  12.5 us
  transfers between devices with their start and end apart: 5, of which 5 were waited for; matrix products, arithmetic and copies ran while one was open for 0% of the time, Pallas kernels for 0%

commit v1 on v0

--- a/solution.py
+++ b/solution.py
@@ -96,7 +96,8 @@
     ).astype(jnp.float32)
     tentative = jnp.dot(weighted, onehot, precision=highest)
     part = part + tentative.reshape(nrhs, pblocks, width).transpose(1, 0, 2)
-    coarse = lax.psum(part, "col")
+    pieces = lax.all_gather(part, "col", axis=0, tiled=False)
+    coarse = pieces.sum(axis=0)
     return (relaxed_iterate[None, None], residual[None, None], coarse[None])
 
 

time: 541 us -> 507 us (0.937)
  blocking collectives: 82.6 us -> 47.6 us
    psum x1 -> x0, blocking collectives: 82.6 us -> none  [body(): coarse = lax.psum(part, 'col')]
    all_gather x0 -> x1, blocking collectives: none -> 47.6 us  [body(): pieces = lax.all_gather(part, 'col', axis=0, tiled=False)]
where the time goes in v1:
time: 507 us; the launch traced here: 505 us
  waiting for transfers between devices  395 us (78%)
  blocking collectives  47.6 us (9%)
  matrix products  19.1 us (4%)
  local copies, waits for them, and re-layouts  18.2 us (4%)
  between operations  15.3 us (3%)
  other arithmetic  9.98 us (2%)
    all_gather x3, waiting for transfers between devices, gather_columns(): whole = lax.all_gather(vec[None, None], 'row', axis=0, tiled=True)  212 us
    reduce_scatter x2, waiting for transfers between devices, stiffness_product(): lax.psum_scatter(partial_value, 'col', scatter_dimension=1, tiled=True)  182 us
    all_gather x1, blocking collectives, body(): pieces = lax.all_gather(part, 'col', axis=0, tiled=False)  47.6 us
    gather x7, local copies, waits for them, and re-layouts, add_group(): inputs = jnp.take(blocks, col_ids, axis=0)  12.5 us
    dot_general x7, matrix products, add_group(): product = jnp.einsum('ska,sab->skb', inputs, piece, precision=highest)  10.5 us
  transfers between devices with their start and end apart: 5, of which 5 were waited for; matrix products, arithmetic and copies ran while one was open for 0% of the time, Pallas kernels for 0%

profile of v1, /device:TPU:8, one launch (start us, length us, event | category | flops | bytes accessed | tf_op | source)
XLA Modules:
  0.0 505.5 jit_solution(13876492053143470296)
XLA Ops:
  7.2 0.0 copy-start
  7.2 0.0 all-gather.9.cloned.1.call-start
  7.2 0.8 copy-done
  8.1 1.6 convolution_multiply_fusion.1
  9.7 0.0 all-gather.9.cloned.1.call-update
  9.7 0.0 reduce-scatter.3.cloned.1.call-start
  10.4 76.2 %all-gather.9.cloned.1.call-done = f32[64,32,128]{2,1,0:T(8,128)} async-done(((f32[2,32,128]{2,1,0:T(8,128)}), f32[64,32,128]{2,1,0:T(8,128)}) %all-gather.9.cloned.1.call-update) | async-done | bytes 1048592 | tf_op jit(solution)/shard_map/all_gather | solution.py:34
  86.7 19.1 %while.30 = (s32[]{:T(128)}, f32[32,32,128]{2,0,1:T(8,128)S(1)}, s32[]{:T(128)}, s32[32]{0:T(128)}, s32[]{:T(128)}, /*index=5*/s32[32]{0:T(128)}, f32[64,32,128]...) while((s32[]{:T(128)}, f32[32,32,128]{2,0,1:T(8,128)S(1)}, ...), condition=%wide.region_1.3_spmd, body=%wide.region_0.2_spmd.sunk | while | flops 63080028 | bytes 2232807 | solution.py:30
  86.7 1.4 compare_and_fusion.6
  88.1 1.8 gather_fusion
  89.9 1.7 fusion.74
  91.6 0.7 dynamic_slice.46
  92.3 0.8 convolution_add_fusion.6
  93.1 1.4 compare_and_fusion.6
  94.5 1.8 gather_fusion
  96.3 1.7 fusion.74
  97.9 0.7 dynamic_slice.46
  98.7 0.8 convolution_add_fusion.6
  99.5 1.4 compare_and_fusion.6
  100.9 1.8 gather_fusion
  102.7 1.7 fusion.74
  104.3 0.7 dynamic_slice.46
  105.0 0.8 convolution_add_fusion.6
  105.9 1.1 copy.25
  107.0 0.0 reduce-scatter.3.cloned.1.call-update
  107.0 0.0 all-gather.11.cloned.1.call-start
  107.1 91.7 %reduce-scatter.3.cloned.1.call-done = f32[1,1,2,32,128]{4,3,2,1,0:T(8,128)} async-done(((f32[1,16,2,32,128]{4,3,2,1,0:T(8,128)}), f32[1,1,2,32,128]{4,3,2,1,0:T(8,128)}) %reduce-scatter.3.cloned.1.call-update) | async-done | bytes 32784 | tf_op jit(solution)/shard_map/reduce_scatter | solution.py:49
  198.8 1.6 fusion.44
  200.4 0.0 all-gather.11.cloned.1.call-update
  200.4 0.0 reduce-scatter.5.cloned.1.call-start
  200.5 68.7 %all-gather.11.cloned.1.call-done = f32[64,32,128]{2,1,0:T(8,128)} async-done(((f32[2,32,128]{2,1,0:T(8,128)}), f32[64,32,128]{2,1,0:T(8,128)}) %all-gather.11.cloned.1.call-update) | async-done | bytes 1048592 | tf_op jit(solution)/shard_map/all_gather | solution.py:34
  269.3 15.3 %while.31 = (s32[]{:T(128)}, f32[32,32,128]{2,0,1:T(8,128)S(1)}, s32[]{:T(128)}, s32[32]{0:T(128)S(1)}, s32[]{:T(128)}, /*index=5*/s32[32]{0:T(128)S(1)}, f32[64...) while((s32[]{:T(128)}, f32[32,32,128]{2,0,1:T(8,128)S(1)}, ...), condition=%wide.region_4.6_spmd, body=%wide.region_3.5_spmd.sunk | while | flops 63080028 | bytes 2232807 | solution.py:30
  269.3 0.8 compare_and_fusion.7
  270.2 1.8 gather_fusion.1
  271.9 1.7 fusion.79
  273.6 0.1 dynamic_slice.48
  273.7 0.8 convolution_add_fusion.7
  274.5 0.7 compare_and_fusion.7
  275.2 1.8 gather_fusion.1
  277.0 1.7 fusion.79
  278.7 0.1 dynamic_slice.48
  278.7 0.8 convolution_add_fusion.7
  279.6 0.7 compare_and_fusion.7
  280.3 1.8 gather_fusion.1
  282.1 1.7 fusion.79
  283.7 0.1 dynamic_slice.48
  283.8 0.8 convolution_add_fusion.7
  284.6 1.1 copy.26
  285.7 0.0 reduce-scatter.5.cloned.1.call-update
  285.8 0.0 all-gather.7.cloned.1.call-start
  285.8 90.4 %reduce-scatter.5.cloned.1.call-done = f32[1,1,2,32,128]{4,3,2,1,0:T(8,128)} async-done(((f32[1,16,2,32,128]{4,3,2,1,0:T(8,128)}), f32[1,1,2,32,128]{4,3,2,1,0:T(8,128)}) %reduce-scatter.5.cloned.1.call-update) | async-done | bytes 32784 | tf_op jit(solution)/shard_map/reduce_scatter | solution.py:49
  376.2 1.4 sub.30
  377.6 0.0 all-gather.7.cloned.1.call-update
  378.3 0.8 fusion.51
  379.2 67.5 %all-gather.7.cloned.1.call-done = f32[32,1,2,32,128]{4,3,2,1,0:T(8,128)} async-done(((f32[1,1,2,32,128]{4,3,2,1,0:T(8,128)}), f32[32,1,2,32,128]{4,3,2,1,0:T(8,128)}) %all-gather.7.cloned.1.call-update) | async-done | bytes 1048592 | tf_op jit(solution)/shard_map/all_gather | solution.py:34
  446.8 3.6 while.32
  446.8 0.7 compare_and_fusion.8
  447.5 1.8 gather_fusion.2
  449.3 0.6 fusion.84
  449.9 0.1 dynamic_slice.50
  450.0 0.3 convolution_add_fusion.8
  450.4 0.3 fusion.43
  450.7 47.6 %all-gather.2 = f32[32,32,128]{2,1,0:T(8,128)S(1)} all-gather(f32[2,32,128]{2,1,0:T(8,128)S(1)} %fusion.43), channel_id=4, replica_groups=mesh['row'=32,'col'=16] {'col'}, dimensions={0}, use_global_device_ids=true | all-gather | bytes 557056 | tf_op jit(solution)/shard_map/all_gather | solution.py:99
  498.3 0.6 reduce_sum.9
  (31 shorter events, 0.3 us)
Async XLA Ops:
  7.2 0.9 copy-start
  7.2 79.4 %all-gather.9.cloned.1.call-start = ((), (), s32[]{:S(2)}) async-start(), calls=%async_computation.5 | async-start | bytes 1081344 | tf_op jit(solution)/shard_map/all_gather | solution.py:34
  9.7 189.1 %reduce-scatter.3.cloned.1.call-start = ((), (), s32[]{:S(2)}) async-start(), calls=%async_computation.2 | async-start | bytes 557056 | tf_op jit(solution)/shard_map/reduce_scatter | solution.py:49
  86.7 112.1 %copy-start.2 = (f32[1,1,2,32,128]{4,3,2,1,0:T(8,128)S(1)}, f32[1,1,2,32,128]{4,3,2,1,0:T(8,128)}, u32[]{:S(2)}) copy-start(f32[1,1,2,32,128]{4,3,2,1,0:T(8,128)} %param.20) | copy-start | bytes 98308
  86.7 112.1 %copy-start.3 = (f32[2,32,128]{2,1,0:T(8,128)S(1)}, f32[2,32,128]{2,1,0:T(8,128)}, u32[]{:S(2)}) copy-start(f32[2,32,128]{2,1,0:T(8,128)} %convolution_multiply_fusion.1) | copy-start | bytes 98308
  105.8 163.4 %copy-start.4 = (s32[32]{0:T(128)S(1)}, s32[32]{0:T(128)}, u32[]{:S(2)}) copy-start(s32[32]{0:T(128)} %get-tuple-element.489) | copy-start | bytes 388
  105.9 163.4 %copy-start.8 = (s32[32]{0:T(128)S(1)}, s32[32]{0:T(128)}, u32[]{:S(2)}) copy-start(s32[32]{0:T(128)} %get-tuple-element.491) | copy-start | bytes 388
  107.0 162.2 %all-gather.11.cloned.1.call-start = ((), (), s32[]{:S(2)}) async-start(), calls=%async_computation.6 | async-start | bytes 1081344 | tf_op jit(solution)/shard_map/all_gather | solution.py:34
  200.4 175.8 %reduce-scatter.5.cloned.1.call-start = ((), (), s32[]{:S(2)}) async-start(), calls=%async_computation.3 | async-start | bytes 557056 | tf_op jit(solution)/shard_map/reduce_scatter | solution.py:49
  269.3 109.0 %copy-start.6 = (f32[1,1,2,128]{3,2,1,0:T(2,128)S(1)}, f32[1,1,2,128]{3,2,1,0:T(2,128)}, u32[]{:S(2)}) copy-start(f32[1,1,2,128]{3,2,1,0:T(2,128)} %param.30) | copy-start | bytes 3076
  269.3 177.4 %copy-start.1 = (f32[1,1,16,128,128]{4,3,2,1,0:T(8,128)S(1)}, f32[1,1,16,128,128]{4,3,2,1,0:T(8,128)}, u32[]{:S(2)}) copy-start(f32[1,1,16,128,128]{4,3,2,1,0:T(8,128)} %param.26) | copy-start | bytes 3145732
  269.3 177.4 %copy-start.5 = (s32[1,1,16]{2,1,0:T(1,128)S(1)}, s32[1,1,16]{2,1,0:T(1,128)}, u32[]{:S(2)}) copy-start(s32[1,1,16]{2,1,0:T(1,128)} %param.28) | copy-start | bytes 196
  269.3 177.4 %copy-start.9 = (s32[1,1,16]{2,1,0:T(1,128)S(1)}, s32[1,1,16]{2,1,0:T(1,128)}, u32[]{:S(2)}) copy-start(s32[1,1,16]{2,1,0:T(1,128)} %param.27) | copy-start | bytes 196
  285.8 160.9 %all-gather.7.cloned.1.call-start = ((), (), s32[]{:S(2)}) async-start(), calls=%async_computation.4 | async-start | bytes 1081344 | tf_op jit(solution)/shard_map/all_gather | solution.py:34
  446.7 3.6 copy-start.7
Sparse Core Ops, SparseCore 0:
  11.7 74.8 all-gather.8
  107.1 91.6 reduce-scatter.2
  202.5 66.6 all-gather.10
  285.9 90.2 reduce-scatter.4
  379.8 66.8 all-gather.6
